TPU v7x, 256 devices: a whole 4x4x8 slice. The times are simulated.
256 devices in a mesh: gx: 16 (over z, core), gy: 4 (over x), member: 4 (over y).
Axes of the slice: x: 4, y: 4, z: 8, core: 2. Of those that a mesh axis runs over, the one named last changes fastest.
Arguments:
- density: float32 [4, 64, 128, 256], P('member', 'gx', 'gy'), may hold values from 0.5 to 1.5
- velocity: float32 [4, 3, 64, 128, 256], P('member', None, 'gx', 'gy'), may hold values from -0.5 to 0.5
- pressure: float32 [4, 64, 128, 256], P('member', 'gx', 'gy'), may hold values from 0.5 to 1.5
- start_block: float32 [4, 128, 16], P('member'), may hold values from -6 to 6
- test_vectors: float32 [32, 64, 128], P('gx', 'gy'), may hold values from -48 to 48
Outputs:
- state_next: float32 [4, 5, 64, 128, 256], P('member', None, 'gx', 'gy')
- projected: float32 [32, 64, 128], P('gx', 'gy')
All inputs are finite; a program needn't handle non-finite values.
Results may differ from a plain program's by a relative error of at most 0.00013.
Values sent between devices are 32-bit elements; how exact they have to be, the bound alone decides.
A program may use at most 64 MiB of HBM per device.

v0:
```python
import jax
import jax.numpy as jnp
from jax import lax
from jax.sharding import PartitionSpec as P

HEAT_RATIO = 1.4
TIME_STEP = 0.08
PRECISE = lax.Precision.HIGHEST


def padded(block, sides, width):
    for axis, dim in sides:
        count = lax.axis_size(axis)
        forward = [(i, i + 1) for i in range(count - 1)]
        forward.append((count - 1, 0))
        backward = [(target, source) for source, target in forward]
        low = lax.ppermute(
            lax.slice_in_dim(block, block.shape[dim] - width, None, axis=dim), axis, forward
        )
        high = lax.ppermute(lax.slice_in_dim(block, 0, width, axis=dim), axis, backward)
        block = jnp.concatenate([low, block, high], axis=dim)
    return block


def cut(values, dimension, start_at, stop_at):
    return lax.slice_in_dim(values, start_at, stop_at, axis=dimension)


def conserved(density, velocity, pressure):
    momentum = density[None] * velocity
    energy = pressure / (HEAT_RATIO - 1.0) + 0.5 * density * jnp.sum(velocity * velocity, axis=0)
    return jnp.concatenate([density[None], momentum, energy[None]], axis=0)


def primitive(fields):
    velocity = fields[1:4] / fields[0]
    kinetic = 0.5 * jnp.sum(fields[1:4] * velocity, axis=0)
    pressure = (HEAT_RATIO - 1.0) * (fields[4] - kinetic)
    sound_speed = jnp.sqrt(HEAT_RATIO * pressure / fields[0])
    return (velocity, pressure, sound_speed)


def directed(fields, velocity, pressure, sound_speed, direction):
    normal = velocity[direction]
    components = [fields[1 + direction]]
    for component in range(3):
        moment_flux = fields[1 + component] * normal
        if component == direction:
            moment_flux = moment_flux + pressure
        components.append(moment_flux)
    components.append((fields[4] + pressure) * normal)
    return (jnp.stack(components), jnp.abs(normal) + sound_speed)


def tendency(fields):
    velocity, pressure, sound_speed = primitive(fields)
    summed = None
    for direction in range(3):
        fluxes, wave_speed = directed(fields, velocity, pressure, sound_speed, direction)
        if direction < 2:
            dimension = 1 + direction
            extent = fields.shape[dimension]
            left_flux = cut(fluxes, dimension, 0, extent - 1)
            right_flux = cut(fluxes, dimension, 1, extent)
            left_fields = cut(fields, dimension, 0, extent - 1)
            right_fields = cut(fields, dimension, 1, extent)
            bound_speed = jnp.maximum(
                cut(wave_speed, dimension - 1, 0, extent - 1),
                cut(wave_speed, dimension - 1, 1, extent),
            )
        else:
            left_flux = fluxes
            right_flux = jnp.roll(fluxes, -1, axis=3)
            left_fields = fields
            right_fields = jnp.roll(fields, -1, axis=3)
            bound_speed = jnp.maximum(wave_speed, jnp.roll(wave_speed, -1, axis=2))
        face_flux = 0.5 * (left_flux + right_flux) - 0.5 * bound_speed * (
            right_fields - left_fields
        )
        if direction < 2:
            change = cut(face_flux, dimension, 1, extent - 1) - cut(
                face_flux, dimension, 0, extent - 2
            )
            cross_dim = 2 - direction
            change = cut(change, cross_dim, 1, change.shape[cross_dim] - 1)
        else:
            change = face_flux - jnp.roll(face_flux, 1, axis=3)
            change = change[:, 1:-1, 1:-1]
        summed = change if summed is None else summed + change
    return -summed


def ghosted(fields):
    return padded(fields, (("gx", 1), ("gy", 2)), 1)


def shards(density, velocity, pressure, start_block, test_vectors):
    fields = conserved(density[0], velocity[0], pressure[0])
    section_one = fields + TIME_STEP * tendency(ghosted(fields))
    second = 0.5 * fields + 0.5 * (section_one + TIME_STEP * tendency(ghosted(section_one)))
    sampled = second[0, ::2, ::2, ::2]
    flattened = sampled.reshape(-1, sampled.shape[2])
    matrix = flattened - jnp.mean(flattened, axis=1, keepdims=True)
    sketch = jnp.dot(matrix, start_block[0], precision=PRECISE)
    folded = lax.psum(jnp.dot(matrix.T, sketch, precision=PRECISE), ("gx", "gy"))
    member_basis = jnp.dot(matrix, folded, precision=PRECISE)
    stacked = lax.all_gather(member_basis, "member", axis=1, tiled=True)
    vectors = test_vectors.reshape(-1, test_vectors.shape[2])
    gram_matrix, cross_terms = lax.psum(
        (
            jnp.dot(stacked.T, stacked, precision=PRECISE),
            jnp.dot(stacked.T, vectors, precision=PRECISE),
        ),
        ("gx", "gy"),
    )
    factor = jnp.linalg.cholesky(gram_matrix)
    halfway = lax.linalg.triangular_solve(factor, cross_terms, left_side=True, lower=True)
    coefficients = lax.linalg.triangular_solve(
        factor, halfway, left_side=True, lower=True, transpose_a=True
    )
    projected = jnp.dot(stacked, coefficients, precision=PRECISE).reshape(test_vectors.shape)
    return (second[None], projected)


def solution(mesh):
    return jax.shard_map(
        shards,
        mesh=mesh,
        in_specs=(
            P("member", "gx", "gy", None),
            P("member", None, "gx", "gy", None),
            P("member", "gx", "gy", None),
            P("member", None, None),
            P("gx", "gy", None),
        ),
        out_specs=(P("member", None, "gx", "gy", None), P("gx", "gy", None)),
        check_vma=False,
    )
```

profile of v0, /device:TPU:8, one launch (start us, length us, event | category | flops | bytes accessed | tf_op | source)
XLA Modules:
  0.0 563.6 jit_solution(3329118583548477129)
XLA Ops:
  0.7 1.1 bitcast_multiply_fusion.1
  1.8 1.0 fusion.45
  2.9 5.3 collective-permute-start.1
  8.2 3.0 collective-permute-done
  11.3 1.6 collective-permute-start.2
  12.8 1.7 collective-permute-start.3
  14.6 1.9 collective-permute-done.2
  18.4 0.4 slice.397
  19.2 0.4 fusion.3
  19.9 0.9 slice-done
  20.7 0.7 fusion.6
  21.7 0.6 fusion.28
  22.3 2.9 collective-permute-start.5
  25.3 3.0 collective-permute-done.4
  28.3 1.6 collective-permute-start.6
  29.9 1.7 collective-permute-start.7
  31.6 1.9 collective-permute-done.6
  35.0 0.4 slice.431
  35.5 0.4 slice.435
  36.3 0.4 fusion.1
  36.9 0.9 slice-done.1
  37.8 0.8 fusion.10
  38.8 0.6 fusion.23
  39.4 0.7 slice.363
  40.9 250.3 %psum.21 = f32[128,16]{1,0:T(8,128)S(1)} all-reduce(f32[128,16]{1,0:T(8,128)S(1)} %fusion.62), channel_id=1, replica_groups=mesh['gx'=16,'gy'=4,'member'=4] {'gx','gy'}, use_global_device_ids=true, to_apply=%region_4.5 | all-reduce | flops 2048 | bytes 16384 | tf_op jit(solution)/shard_map/psum | solution.py:105
  291.4 12.2 %all_gather.3 = f32[32,64]{0,1:T(8,128)S(1)} all-gather(f32[32,16]{0,1:T(8,128)S(1)} %fusion.63), channel_id=1, replica_groups=mesh['gx'=16,'gy'=4,'member'=4] {'member'}, dimensions={1}, use_global_device_ids=true | all-gather | bytes 10240 | tf_op jit(solution)/shard_map/all_gather | solution.py:107
  304.0 246.2 %all-reduce = (f32[64,128]{1,0:T(8,128)S(1)}, f32[64,64]{0,1:T(8,128)S(1)}) all-reduce(f32[64,128]{1,0:T(8,128)S(1)} %fusion.65, f32[64,64]{0,1:T(8,128)S(1)} %fusion.64), channel_id=1, replica_groups=mesh['gx'=16,'gy'=4,'member'=4] {'gx','gy'}, use_global_device_ids=true, to_apply=%region_8.9 | all-reduce | flops 12288 | bytes 98304 | tf_op jit(solution)/shard_map/psum | solution.py:109
  550.2 5.8 %cholesky.16 = f32[64,64]{1,0:T(8,128)S(1)} custom-call(f32[64,64]{1,0:T(8,128)S(1)} %fusion.51), custom_call_target="Cholesky" | custom-call | tf_op jit(solution)/shard_map/jit(cholesky)/cholesky | solution.py:116
  556.1 0.6 compare_reduce_fusion
  556.7 0.7 fusion.46
  557.4 4.9 custom-call.8
  562.7 0.8 fusion.66
  (83 shorter events, 7.2 us)
Async XLA Ops:
  0.6 303.2 %copy-start = (f32[2,16,128]{2,1,0:T(8,128)S(1)}, f32[2,16,128]{2,1,0:T(8,128)}, u32[]{:S(2)}) copy-start(f32[2,16,128]{2,1,0:T(8,128)} %param.9) | copy-start | bytes 49156
  0.6 2.1 copy-start.3
  2.9 8.3 %collective-permute-start = (f32[5,1,32,256]{3,2,1,0:T(8,128)S(1)}, f32[5,1,32,256]{3,2,1,0:T(8,128)S(1)}, u32[]{:S(2)}, u32[]{:S(2)}) collective-permute-start(f32[5,1,32,256]{3,2,1,0:T(8,128)S(1)} %get-tuple-element.62), channel_id=1, source_target_pairs={{0,16},{16,32},{32,48},{48,64},{64,80},{80,96},{96,112},{112,128},... | collective-permute-start | bytes 491528 | tf_op jit(solution)/shard_map/ppermute | solution.py:17
  2.9 8.3 %collective-permute-start.1 = (f32[5,1,32,256]{3,2,1,0:T(8,128)S(1)}, f32[5,1,32,256]{3,2,1,0:T(8,128)S(1)}, u32[]{:S(2)}, u32[]{:S(2)}) collective-permute-start(f32[5,1,32,256]{3,2,1,0:T(8,128)S(1)} %get-tuple-element.63), channel_id=1, source_target_pairs={{16,0},{32,16},{48,32},{64,48},{80,64},{96,80},{112,96},{128,112},... | collective-permute-start | bytes 491528 | tf_op jit(solution)/shard_map/ppermute | solution.py:20
  11.3 5.2 collective-permute-start.2
  12.8 3.9 collective-permute-start.3
  16.9 1.9 copy-start.1
  19.6 1.1 slice-start
  22.3 6.0 %collective-permute-start.4 = (f32[5,1,32,256]{3,2,1,0:T(8,128)S(1)}, f32[5,1,32,256]{3,2,1,0:T(8,128)S(1)}, u32[]{:S(2)}, u32[]{:S(2)}) collective-permute-start(f32[5,1,32,256]{3,2,1,0:T(8,128)S(1)} %get-tuple-element.60), channel_id=1, source_target_pairs={{0,16},{16,32},{32,48},{48,64},{64,80},{80,96},{96,112},{112,128},... | collective-permute-start | bytes 491528 | tf_op jit(solution)/shard_map/ppermute | solution.py:17
  22.3 5.9 %collective-permute-start.5 = (f32[5,1,32,256]{3,2,1,0:T(8,128)S(1)}, f32[5,1,32,256]{3,2,1,0:T(8,128)S(1)}, u32[]{:S(2)}, u32[]{:S(2)}) collective-permute-start(f32[5,1,32,256]{3,2,1,0:T(8,128)S(1)} %get-tuple-element.61), channel_id=1, source_target_pairs={{16,0},{32,16},{48,32},{64,48},{80,64},{96,80},{112,96},{128,112},... | collective-permute-start | bytes 491528 | tf_op jit(solution)/shard_map/ppermute | solution.py:20
  28.3 5.2 collective-permute-start.6
  29.9 3.9 collective-permute-start.7
  33.9 1.9 copy-start.2
  36.7 1.1 slice-start.1
  38.8 1.7 copy-start.5
  39.4 524.1 %copy-start.4 = (f32[5,4,32,256]{3,2,1,0:T(8,128)}, f32[5,4,32,256]{3,2,1,0:T(8,128)S(1)}, u32[]{:S(2)}) copy-start(f32[5,4,32,256]{3,2,1,0:T(8,128)S(1)} %fusion.23) | copy-start | bytes 1966084
where the time goes:
time: 564 us
  blocking collectives  509 us (90%)
  other arithmetic  20.6 us (4%)
  starting transfers between devices  14.9 us (3%)
  waiting for transfers between devices  10.3 us (2%)
  local copies, waits for them, and re-layouts  5.75 us (1%)
    psum x1, blocking collectives, shards(): lax.psum(jnp.dot(matrix.T, sketch, precision=PRECISE), ('gx', 'gy'))  250 us
    psum x1, blocking collectives, shards(): lax.psum((jnp.dot(stacked.T, stacked, precision=PRECISE), jnp.dot(stacked...  246 us
    all_gather x1, blocking collectives, shards(): stacked = lax.all_gather(member_basis, 'member', axis=1, tiled=True)  12.2 us
    ppermute x4, starting transfers between devices, padded(): lax.ppermute(lax.slice_in_dim(block, 0, width, axis=dim), axis, backward)  11.7 us
  transfers between devices with their start and end apart: 8, of which 6 were waited for; matrix products, arithmetic and copies ran while one was open for 0% of the time, Pallas kernels for 0%

commit v1 on v0

--- a/solution.py
+++ b/solution.py
@@ -102,7 +102,9 @@
     flattened = sampled.reshape(-1, sampled.shape[2])
     matrix = flattened - jnp.mean(flattened, axis=1, keepdims=True)
     sketch = jnp.dot(matrix, start_block[0], precision=PRECISE)
-    folded = lax.psum(jnp.dot(matrix.T, sketch, precision=PRECISE), ("gx", "gy"))
+    folded = jnp.sum(
+        lax.all_gather(jnp.dot(matrix.T, sketch, precision=PRECISE), ("gx", "gy")), axis=0
+    )
     member_basis = jnp.dot(matrix, folded, precision=PRECISE)
     stacked = lax.all_gather(member_basis, "member", axis=1, tiled=True)
     vectors = test_vectors.reshape(-1, test_vectors.shape[2])

time: 564 us -> 387 us (0.69)
  blocking collectives: 509 us -> 332 us
    psum x1 -> x0, blocking collectives: 250 us -> none  [shards(): lax.psum(jnp.dot(matrix.T, sketch, precision=PRECISE), ('gx', 'gy'))]
    all_gather x0 -> x1, blocking collectives: none -> 72.8 us  [shards(): lax.all_gather(jnp.dot(matrix.T, sketch, precision=PRECISE), ('gx', 'gy'))]
where the time goes in v1:
time: 387 us
  blocking collectives  332 us (86%)
  other arithmetic  20.7 us (5%)
  starting transfers between devices  14.9 us (4%)
  waiting for transfers between devices  10.3 us (3%)
  local copies, waits for them, and re-layouts  5.86 us (2%)
    psum x1, blocking collectives, shards(): lax.psum((jnp.dot(stacked.T, stacked, precision=PRECISE), jnp.dot(stacked...  247 us
    all_gather x1, blocking collectives, shards(): lax.all_gather(jnp.dot(matrix.T, sketch, precision=PRECISE), ('gx', 'gy'))  72.8 us
    all_gather x1, blocking collectives, shards(): stacked = lax.all_gather(member_basis, 'member', axis=1, tiled=True)  12.2 us
    ppermute x4, starting transfers between devices, padded(): lax.ppermute(lax.slice_in_dim(block, 0, width, axis=dim), axis, backward)  11.7 us
    ppermute x4, waiting for transfers between devices, padded(): lax.ppermute(lax.slice_in_dim(block, block.shape[dim] - width, None, axis...  9.71 us
  transfers between devices with their start and end apart: 8, of which 6 were waited for; matrix products, arithmetic and copies ran while one was open for 0% of the time, Pallas kernels for 0%

profile of v1, /device:TPU:8, one launch (start us, length us, event | category | flops | bytes accessed | tf_op | source)
XLA Modules:
  0.0 386.9 jit_solution(15764909479835458316)
XLA Ops:
  0.7 1.1 bitcast_multiply_fusion.1
  1.8 1.0 fusion.45
  2.9 5.3 %collective-permute-start.1 = (f32[5,1,32,256]{3,2,1,0:T(8,128)S(1)}, f32[5,1,32,256]{3,2,1,0:T(8,128)S(1)}, u32[]{:S(2)}, u32[]{:S(2)}) collective-permute-start(f32[5,1,32,256]{3,2,1,0:T(8,128)S(1)} %get-tuple-element.63), channel_id=1, source_target_pairs={{16,0},{32,16},{48,32},{64,48},{80,64},{96,80},{112,96},{128,112},... | collective-permute-start | bytes 491528 | tf_op jit(solution)/shard_map/ppermute | solution.py:20
  8.2 3.0 collective-permute-done
  11.3 1.6 collective-permute-start.2
  12.8 1.7 collective-permute-start.3
  14.6 1.9 collective-permute-done.2
  18.4 0.4 slice.397
  19.2 0.4 fusion.3
  19.9 0.9 slice-done
  20.7 0.7 fusion.6
  21.7 0.6 fusion.28
  22.3 2.9 collective-permute-start.5
  25.3 3.0 collective-permute-done.4
  28.3 1.6 collective-permute-start.6
  29.9 1.7 collective-permute-start.7
  31.6 1.9 collective-permute-done.6
  35.0 0.4 slice.431
  35.5 0.4 slice.435
  36.3 0.4 fusion.1
  36.9 0.9 slice-done.1
  37.8 0.8 fusion.10
  38.8 0.6 fusion.23
  39.4 0.7 slice.363
  40.8 72.8 %all-gather = f32[8192,16]{0,1:T(8,128)S(1)} all-gather(f32[128,16]{0,1:T(8,128)S(1)} %fusion.62), channel_id=2, replica_groups=mesh['gx'=16,'gy'=4,'member'=4] {'gx','gy'}, dimensions={0}, use_global_device_ids=true | all-gather | bytes 532480 | tf_op jit(solution)/shard_map/all_gather | solution.py:106
  113.9 12.2 %all_gather.11 = f32[32,64]{0,1:T(8,128)S(1)} all-gather(f32[32,16]{0,1:T(8,128)S(1)} %fusion.63), channel_id=1, replica_groups=mesh['gx'=16,'gy'=4,'member'=4] {'member'}, dimensions={1}, use_global_device_ids=true | all-gather | bytes 10240 | tf_op jit(solution)/shard_map/all_gather | solution.py:109
  126.4 247.1 %all-reduce = (f32[64,128]{1,0:T(8,128)S(1)}, f32[64,64]{0,1:T(8,128)S(1)}) all-reduce(f32[64,128]{1,0:T(8,128)S(1)} %fusion.65, f32[64,64]{0,1:T(8,128)S(1)} %fusion.64), channel_id=1, replica_groups=mesh['gx'=16,'gy'=4,'member'=4] {'gx','gy'}, use_global_device_ids=true, to_apply=%region_8.9 | all-reduce | flops 12288 | bytes 98304 | tf_op jit(solution)/shard_map/psum | solution.py:111
  373.5 5.8 %cholesky.16 = f32[64,64]{1,0:T(8,128)S(1)} custom-call(f32[64,64]{1,0:T(8,128)S(1)} %fusion.51), custom_call_target="Cholesky" | custom-call | tf_op jit(solution)/shard_map/jit(cholesky)/cholesky | solution.py:118
  379.4 0.6 compare_reduce_fusion
  380.1 0.7 fusion.46
  380.7 4.9 %custom-call.8 = f32[1,64,64]{1,2,0:T(8,128)S(1)} custom-call(f32[1,64,64]{2,1,0:T(8,128)S(1)} %fusion.46), custom_call_target="InvertDiagBlocksLowerTriangular" | custom-call | tf_op jit(solution)/shard_map/triangular_solve | solution.py:120
  386.1 0.8 fusion.66
  (85 shorter events, 7.1 us)
Async XLA Ops:
  0.6 125.6 %copy-start = (f32[2,16,128]{2,1,0:T(8,128)S(1)}, f32[2,16,128]{2,1,0:T(8,128)}, u32[]{:S(2)}) copy-start(f32[2,16,128]{2,1,0:T(8,128)} %param.9) | copy-start | bytes 49156
  0.6 2.1 copy-start.3
  2.9 8.3 %collective-permute-start = (f32[5,1,32,256]{3,2,1,0:T(8,128)S(1)}, f32[5,1,32,256]{3,2,1,0:T(8,128)S(1)}, u32[]{:S(2)}, u32[]{:S(2)}) collective-permute-start(f32[5,1,32,256]{3,2,1,0:T(8,128)S(1)} %get-tuple-element.62), channel_id=1, source_target_pairs={{0,16},{16,32},{32,48},{48,64},{64,80},{80,96},{96,112},{112,128},... | collective-permute-start | bytes 491528 | tf_op jit(solution)/shard_map/ppermute | solution.py:17
  2.9 8.3 %collective-permute-start.1 = (f32[5,1,32,256]{3,2,1,0:T(8,128)S(1)}, f32[5,1,32,256]{3,2,1,0:T(8,128)S(1)}, u32[]{:S(2)}, u32[]{:S(2)}) collective-permute-start(f32[5,1,32,256]{3,2,1,0:T(8,128)S(1)} %get-tuple-element.63), channel_id=1, source_target_pairs={{16,0},{32,16},{48,32},{64,48},{80,64},{96,80},{112,96},{128,112},... | collective-permute-start | bytes 491528 | tf_op jit(solution)/shard_map/ppermute | solution.py:20
  11.3 5.2 %collective-permute-start.2 = (f32[5,6,1,256]{3,2,1,0:T(1,128)S(1)}, f32[5,6,1,256]{3,2,1,0:T(1,128)S(1)}, u32[]{:S(2)}, u32[]{:S(2)}) collective-permute-start(f32[5,6,1,256]{3,2,1,0:T(1,128)S(1)} %get-tuple-element.58), channel_id=1, source_target_pairs={{0,4},{4,8},{8,12},{12,0},{1,5},{5,9},{9,13},{13,1},{2,6},{6,10},{... | collective-permute-start | bytes 92168 | tf_op jit(solution)/shard_map/ppermute | solution.py:17
  12.8 3.9 %collective-permute-start.3 = (f32[5,6,1,256]{3,2,1,0:T(1,128)S(1)}, f32[5,6,1,256]{3,2,1,0:T(1,128)S(1)}, u32[]{:S(2)}, u32[]{:S(2)}) collective-permute-start(f32[5,6,1,256]{3,2,1,0:T(1,128)S(1)} %get-tuple-element.59), channel_id=1, source_target_pairs={{4,0},{8,4},{12,8},{0,12},{5,1},{9,5},{13,9},{1,13},{6,2},{10,6},{... | collective-permute-start | bytes 92168 | tf_op jit(solution)/shard_map/ppermute | solution.py:20
  16.9 1.9 copy-start.1
  19.6 1.1 slice-start
  22.3 6.0 %collective-permute-start.4 = (f32[5,1,32,256]{3,2,1,0:T(8,128)S(1)}, f32[5,1,32,256]{3,2,1,0:T(8,128)S(1)}, u32[]{:S(2)}, u32[]{:S(2)}) collective-permute-start(f32[5,1,32,256]{3,2,1,0:T(8,128)S(1)} %get-tuple-element.60), channel_id=1, source_target_pairs={{0,16},{16,32},{32,48},{48,64},{64,80},{80,96},{96,112},{112,128},... | collective-permute-start | bytes 491528 | tf_op jit(solution)/shard_map/ppermute | solution.py:17
  22.3 5.9 %collective-permute-start.5 = (f32[5,1,32,256]{3,2,1,0:T(8,128)S(1)}, f32[5,1,32,256]{3,2,1,0:T(8,128)S(1)}, u32[]{:S(2)}, u32[]{:S(2)}) collective-permute-start(f32[5,1,32,256]{3,2,1,0:T(8,128)S(1)} %get-tuple-element.61), channel_id=1, source_target_pairs={{16,0},{32,16},{48,32},{64,48},{80,64},{96,80},{112,96},{128,112},... | collective-permute-start | bytes 491528 | tf_op jit(solution)/shard_map/ppermute | solution.py:20
  28.3 5.2 %collective-permute-start.6 = (f32[5,6,1,256]{3,2,1,0:T(1,128)S(1)}, f32[5,6,1,256]{3,2,1,0:T(1,128)S(1)}, u32[]{:S(2)}, u32[]{:S(2)}) collective-permute-start(f32[5,6,1,256]{3,2,1,0:T(1,128)S(1)} %get-tuple-element.54), channel_id=1, source_target_pairs={{0,4},{4,8},{8,12},{12,0},{1,5},{5,9},{9,13},{13,1},{2,6},{6,10},{... | collective-permute-start | bytes 92168 | tf_op jit(solution)/shard_map/ppermute | solution.py:17
  29.9 3.9 %collective-permute-start.7 = (f32[5,6,1,256]{3,2,1,0:T(1,128)S(1)}, f32[5,6,1,256]{3,2,1,0:T(1,128)S(1)}, u32[]{:S(2)}, u32[]{:S(2)}) collective-permute-start(f32[5,6,1,256]{3,2,1,0:T(1,128)S(1)} %get-tuple-element.55), channel_id=1, source_target_pairs={{4,0},{8,4},{12,8},{0,12},{5,1},{9,5},{13,9},{1,13},{6,2},{10,6},{... | collective-permute-start | bytes 92168 | tf_op jit(solution)/shard_map/ppermute | solution.py:20
  33.9 1.9 copy-start.2
  36.7 1.1 slice-start.1
  38.8 1.7 copy-start.5
  39.4 86.8 %copy-start.4 = (f32[5,4,32,256]{3,2,1,0:T(8,128)}, f32[5,4,32,256]{3,2,1,0:T(8,128)S(1)}, u32[]{:S(2)}) copy-start(f32[5,4,32,256]{3,2,1,0:T(8,128)S(1)} %fusion.23) | copy-start | bytes 1966084
